TPU v7x, 32 devices: a whole 2x2x4 slice. The times are simulated.
32 devices in a mesh: ctx: 8 (over z, x), fsdp: 4 (over y, core).
Axes of the slice: x: 2, y: 2, z: 4, core: 2. Of those that a mesh axis runs over, the one named last changes fastest.
Arguments:
- hidden_in: bfloat16 [4, 1024, 2048], P('fsdp', 'ctx'), may hold values from -6 to 6
- positions: int32 [4, 1024], P('fsdp'), may hold values from 0 to 1023, as said below
- ln_gain: bfloat16 [2048], P(('ctx', 'fsdp')), may hold values from 0.25 to 1.75
- ln_bias: bfloat16 [2048], P(('ctx', 'fsdp')), may hold values from -1.75 to 1.75
- w_qkv: bfloat16 [6144, 2048], P(('ctx', 'fsdp')), may hold values from -0.125 to 0.125
- b_qkv: bfloat16 [6144], P(('ctx', 'fsdp')), may hold values from -1.75 to 1.75
- w_dense: bfloat16 [2048, 2048], P(('ctx', 'fsdp')), may hold values from -2 to 2
- b_dense: bfloat16 [2048], P(('ctx', 'fsdp')), may hold values from -1.75 to 1.75
- w_fc1: bfloat16 [8192, 2048], P(('ctx', 'fsdp')), may hold values from -0.125 to 0.125
- b_fc1: bfloat16 [8192], P(('ctx', 'fsdp')), may hold values from -1.75 to 1.75
- w_fc2: bfloat16 [2048, 8192], P(('ctx', 'fsdp')), may hold values from -0.09375 to 0.09375
- b_fc2: bfloat16 [2048], P(('ctx', 'fsdp')), may hold values from -1.75 to 1.75
- out_grad: bfloat16 [4, 1024, 2048], P('fsdp', 'ctx'), may hold values from -6 to 6
Outputs:
- hidden_out: bfloat16 [4, 1024, 2048], P('fsdp', 'ctx')
- grad_in: float32 [4, 1024, 2048], P('fsdp', 'ctx')
- grad_ln_gain: float32 [2048], P(('ctx', 'fsdp'))
- grad_ln_bias: float32 [2048], P(('ctx', 'fsdp'))
- grad_w_qkv: float32 [6144, 2048], P(('ctx', 'fsdp'))
- grad_b_qkv: float32 [6144], P(('ctx', 'fsdp'))
- grad_w_dense: float32 [2048, 2048], P(('ctx', 'fsdp'))
- grad_b_dense: float32 [2048], P(('ctx', 'fsdp'))
- grad_w_fc1: float32 [8192, 2048], P(('ctx', 'fsdp'))
- grad_b_fc1: float32 [8192], P(('ctx', 'fsdp'))
- grad_w_fc2: float32 [2048, 8192], P(('ctx', 'fsdp'))
- grad_b_fc2: float32 [2048], P(('ctx', 'fsdp'))
Inputs may be any that keep to these rules, and one draw needn't show every extreme that they name: For each sequence, stored columns 2 b * 64 to 2 b * 64 + 2 * 64 - 1 hold two runs of 64 consecutive rising positions, one starting at j * 64 and one at (15 - j) * 64, in either order; every position of a sequence appears exactly once.
All inputs are finite; a program needn't handle non-finite values.
Results may differ from a plain program's by a relative error of at most 0.012.
Values may be sent and summed in bfloat16 or wider, within the bound.
A program may use at most 512 MiB of HBM per device.

v0:
```python
import functools

import jax
import jax.numpy as jnp
import numpy as np
from jax import lax
from jax.experimental import pallas as pl
from jax.experimental.pallas import tpu as pltpu
from jax.sharding import PartitionSpec as P

HEAD_DIM = 64
ROT_DIM = 32
RUN = 64
EPSILON = 1e-05
SCORE_SCALE = 0.125
BOTH = ("ctx", "fsdp")
F32 = jnp.float32
LOW = jnp.bfloat16
MESH = pl.DeviceIdType.MESH
SEMAPHORES = 512
VMEM_BYTES = 60 * 1024 * 1024
SMALL_ROWS = (
    [(row, (1, 0)) for row in range(4)]
    + [(4, (3, j)) for j in range(3)]
    + [(7, (4, j)) for j in range(4)]
)


def dot_nt(a, b):
    return lax.dot_general(a, b, (((1,), (1,)), ((), ())), preferred_element_type=F32)


def dot_nn(a, b):
    return lax.dot_general(a, b, (((1,), (0,)), ((), ())), preferred_element_type=F32)


def dot_tn(a, b):
    return lax.dot_general(a, b, (((0,), (0,)), ((), ())), preferred_element_type=F32)


def turning_tables(length):
    half_rot = ROT_DIM // 2
    lane = np.arange(2 * HEAD_DIM) % HEAD_DIM
    freqs = np.where(lane < ROT_DIM, 10000.0 ** (-(lane % half_rot) / half_rot), 0.0)
    starts = np.arange(0, length, RUN)[:, None] * freqs[None, :]
    steps = np.arange(RUN)[:, None] * freqs[None, :]
    return (
        np.stack([np.cos(starts), np.sin(starts)]).astype(np.float32),
        np.stack([np.cos(steps), np.sin(steps)]).astype(np.float32),
    )


def run_turn(start_ref, step_ref, run):
    lane = lax.broadcasted_iota(jnp.int32, (RUN, 2 * HEAD_DIM), 1) % HEAD_DIM
    half_rot = ROT_DIM // 2
    cos_a, sin_a = start_ref[0, pl.ds(run, 1), :], start_ref[1, pl.ds(run, 1), :]
    cos_b, sin_b = step_ref[0], step_ref[1]
    cosine = cos_a * cos_b - sin_a * sin_b
    sine = sin_a * cos_b + cos_a * sin_b
    above = jnp.where(lane < half_rot, -sine, 0.0)
    below = jnp.where((lane >= half_rot) & (lane < ROT_DIM), sine, 0.0)
    return cosine, above, below


def turn(u, tables, way=1.0):
    cosine, above, below = tables
    half_rot = ROT_DIM // 2
    width = 2 * HEAD_DIM
    moved = pltpu.roll(u, width - half_rot, 1) * above + pltpu.roll(u, half_rot, 1) * below
    return u * cosine + way * moved


def masked_tile(scores, diagonal, start):
    last = jnp.where(diagonal, scores[:, start:], -1e30)
    return jnp.concatenate([scores[:, :start], last], axis=1) if start > 0 else last


def lower_triangle(tile):
    return lax.broadcasted_iota(jnp.int32, (tile, tile), 1) <= lax.broadcasted_iota(
        jnp.int32, (tile, tile), 0
    )


def head_lanes(tile, head):
    lanes = lax.broadcasted_iota(jnp.int32, (tile, 2 * HEAD_DIM), 1)
    return (lanes // HEAD_DIM) == head


def pick(mine, values):
    return jnp.where(mine, values, jnp.zeros_like(values))


def attend(q_s, k_s, v_s, ctx_s, lse_s):
    length = q_s.shape[0]
    tile = min(256, length)
    diagonal = lower_triangle(tile)
    for start in range(0, length, tile):
        rows, reach = slice(start, start + tile), start + tile

        @pl.loop(0, 2)
        def _(head, rows=rows, reach=reach, start=start):
            mine = head_lanes(tile, head)
            scores = dot_nt(pick(mine, q_s[rows, :]), k_s[:reach, :])
            scores = masked_tile(scores, diagonal, start)
            peak = jnp.max(scores, axis=1, keepdims=True)
            exps = jnp.exp(scores - peak)
            total = jnp.sum(exps, axis=1, keepdims=True)
            probs_low = (exps * (1.0 / total)).astype(LOW)
            context = dot_nn(probs_low, v_s[:reach, :]).astype(LOW)
            ctx_s[rows, :] = jnp.where(mine, context, ctx_s[rows, :])
            lse_s[rows, :] = jnp.where(mine, peak + jnp.log(total), lse_s[rows, :])


class Grid:
    def __init__(self, ctx_n, fsdp_n):
        self.ctx_n, self.fsdp_n = ctx_n, fsdp_n
        self.x_n = 1 << ((ctx_n.bit_length() - 1) // 2)
        self.z_n = ctx_n // self.x_n
        self.core_n = 2 if fsdp_n % 2 == 0 else 1
        self.y_n = fsdp_n // self.core_n
        self.undo = 1 if ctx_n % 3 == 1 else 2

    def locate(self):
        self.ctx, self.fsdp = lax.axis_index("ctx"), lax.axis_index("fsdp")
        self.z, self.x = self.ctx // self.x_n, self.ctx % self.x_n
        self.y, self.core = self.fsdp // self.core_n, self.fsdp % self.core_n
        return self

    def zx(self, dz, dx):
        return ((self.z + dz + self.z_n) % self.z_n) * self.x_n + (
            self.x + dx + self.x_n
        ) % self.x_n

    def yc(self, dy, dc):
        return ((self.y + dy + self.y_n) % self.y_n) * self.core_n + (
            self.core + dc + self.core_n
        ) % self.core_n

    def nearest(self, j):
        place = 0
        for z in range(self.z_n):
            order = sorted(range(self.z_n), key=lambda other: (abs(other - z), other))
            place = place + jnp.where(self.z == z, order[j], 0)
        return place

    def qkv_piece(self, ctx, fsdp, m):
        span = 3 * self.fsdp_n
        v = (3 * fsdp + m + span * self.ctx_n - ctx * self.fsdp_n) % span
        return ((v // self.fsdp_n) * self.undo) % 3, v % self.fsdp_n

    def qkv_owner(self, ctx, fsdp, m):
        kind, place = self.qkv_piece(ctx, fsdp, m)
        piece = self.ctx_n * self.fsdp_n * kind + ctx * self.fsdp_n + place
        return piece // 3 // self.fsdp_n

    def qkv_user(self, ctx, fsdp, m):
        piece = 3 * (ctx * self.fsdp_n + fsdp) + m
        return (piece % (self.ctx_n * self.fsdp_n)) // self.fsdp_n

    def greet(self):
        barrier = pltpu.get_barrier_semaphore()
        for k in range(1, self.ctx_n):
            pl.semaphore_signal(
                barrier, inc=1, device_id={"ctx": (self.ctx + k) % self.ctx_n}, device_id_type=MESH
            )
        for k in range(1, self.fsdp_n):
            pl.semaphore_signal(
                barrier,
                inc=1,
                device_id={"fsdp": (self.fsdp + k) % self.fsdp_n},
                device_id_type=MESH,
            )
        pl.semaphore_wait(barrier, self.ctx_n + self.fsdp_n - 2)


class Copies:
    def __init__(self, sems):
        self.sems, self.used, self.sent, self.perhaps = sems, 0, [], []

    def sem(self):
        self.used += 1
        return self.sems.at[self.used - 1]

    def send(self, src, dst, **where):
        send_sem, recv_sem = self.sem(), self.sem()
        copy = pltpu.make_async_remote_copy(
            src_ref=src,
            dst_ref=dst,
            send_sem=send_sem,
            recv_sem=recv_sem,
            device_id=where,
            device_id_type=MESH,
        )
        copy.start()
        self.sent.append(copy)
        return recv_sem

    def send_or_keep(self, src, dst, ctx, own_ctx):
        send_sem, recv_sem = self.sem(), self.sem()
        remote = pltpu.make_async_remote_copy(
            src_ref=src,
            dst_ref=dst,
            send_sem=send_sem,
            recv_sem=recv_sem,
            device_id={"ctx": ctx},
            device_id_type=MESH,
        )

        @pl.when(ctx != own_ctx)
        def _():
            remote.start()

        @pl.when(ctx == own_ctx)
        def _():
            pltpu.make_async_copy(src, dst, recv_sem).start()

        self.perhaps.append((ctx != own_ctx, remote))
        return recv_sem

    def prepare(self, src, dst, **where):
        send_sem, recv_sem = self.sem(), self.sem()
        remote = pltpu.make_async_remote_copy(
            src_ref=src,
            dst_ref=dst,
            send_sem=send_sem,
            recv_sem=recv_sem,
            device_id=where,
            device_id_type=MESH,
        )
        return remote, recv_sem

    def start_if(self, when, remote):
        @pl.when(when)
        def _():
            remote.start()

        self.perhaps.append((when, remote))

    def send_if(self, when, src, dst, **where):
        remote, recv_sem = self.prepare(src, dst, **where)
        self.start_if(when, remote)
        return recv_sem

    def local(self, src, dst):
        copy = pltpu.make_async_copy(src, dst, self.sem())
        copy.start()
        return copy

    def drain(self):
        for copy in self.sent:
            copy.wait_send()
        for sent, copy in self.perhaps:

            @pl.when(sent)
            def _(copy=copy):
                copy.wait_send()


def arrived(ref, sem):
    pltpu.make_async_copy(ref, ref, sem).wait()


class TokenGather:
    def __init__(self, grid, copies, own, buffer):
        self.grid, self.copies, self.buffer = grid, copies, buffer
        self.rows = own.shape[0]
        self.across = []
        self.kept = copies.local(own, self.slot(0, 0))
        self.along = {
            way: copies.send_if(self.ends(way), own, self.slot(0, 0), ctx=grid.zx(way, 0))
            for way in (1, -1)
        }
        for l in range(1, grid.x_n):
            sem = copies.send(own, self.slot(0, 0), ctx=grid.zx(0, l))
            self.across.append((0, 1, l, sem))

    def slot(self, k, l):
        start = pl.multiple_of(self.grid.zx(-k, -l) * self.rows, self.rows)
        return self.buffer.at[pl.ds(start, self.rows)]

    def ends(self, way):
        return self.grid.z < self.grid.z_n - 1 if way > 0 else self.grid.z > 0

    def has(self, k, way):
        z = self.grid.z
        return z >= k if way > 0 else z + k < self.grid.z_n

    def step(self, k):
        grid, copies, along = self.grid, self.copies, {}
        for way in (1, -1):
            slot, here = self.slot(k * way, 0), self.has(k, way)

            @pl.when(here)
            def _(slot=slot, way=way):
                arrived(slot, self.along[way])

            if k < grid.z_n - 1:
                along[way] = copies.send_if(
                    here & self.ends(way), slot, slot, ctx=grid.zx(way, 0)
                )
            for l in range(1, grid.x_n):
                sem = copies.send_if(here, slot, slot, ctx=grid.zx(0, l))
                self.across.append((k, way, l, sem))
        self.along = along

    def ready(self, k):
        if k == 0:
            self.kept.wait()
        for m, way, l, sem in self.across:
            if m == k:

                @pl.when(self.has(k, way))
                def _(way=way, l=l, sem=sem):
                    arrived(self.slot(k * way, l), sem)


class ShardGather:
    def __init__(self, grid, copies, own, view):
        self.grid, self.copies, self.view = grid, copies, view
        self.along_y = [
            copies.send(own, view(grid.fsdp), fsdp=grid.yc(k, 0)) for k in range(1, grid.y_n)
        ]
        self.across = []
        self.cross(own, 0)

    def cross(self, src, k):
        for c in range(1, self.grid.core_n):
            slot = self.view(self.grid.yc(-k, 0))
            self.across.append((k, c, self.copies.send(src, slot, fsdp=self.grid.yc(0, c))))

    def forward(self):
        for k in range(1, self.grid.y_n):
            slot = self.view(self.grid.yc(-k, 0))
            arrived(slot, self.along_y[k - 1])
            self.cross(slot, k)

    def finish(self):
        for k, c, sem in self.across:
            arrived(self.view(self.grid.yc(-k, -c)), sem)


def gather_kernel(
    shape, x_in, g_in, wq_in, wu_in, wf_in, wd_in,
    gain_in, shift_in, bd_in, bf_in, bq_in, bu_in, row_in, start_in, step_in,
    x_out, g_out, wi_out, wu_out, wo_out, small_out, normed_out, hidden_out, slope_out,
    qkv_out, lse_out, stats_out,
    x_s, g_s, wi_s, wu_s, wo_s, normed_s, hidden_s, slope_s, qkv_s, lse_s, stats_s,
    mixed_s, ctx_s, small_f, qkv_bias_s, up_bias_s, small_s, small_x, small_core, small_y, small_z, sems,
):
    grid = Grid(*shape).locate()
    copies = Copies(sems)
    local_len, width = x_in.shape
    unit, up_rows = wd_in.shape[0], wu_in.shape[0]
    fw, dw = wf_in.shape[1] // grid.ctx_n, wd_in.shape[1] // grid.ctx_n
    n = grid.ctx_n * grid.fsdp_n
    me = grid.ctx * grid.fsdp_n + grid.fsdp
    peers = [(k, l) for k in range(grid.z_n) for l in range(grid.x_n) if k or l]
    pairs = dw // (2 * HEAD_DIM)
    small_in = gain_in, shift_in, bd_in, bf_in, bq_in, bu_in
    puts = []

    row_index = lax.broadcasted_iota(jnp.int32, (16, width), 0)
    placed = jnp.zeros((16, width), F32)
    small_f[...] = jnp.zeros_like(small_f)
    row = 0
    for piece_in in small_in:
        small_f[row : row + piece_in.shape[0], 0:unit] = piece_in[...].astype(F32)
        row += piece_in.shape[0]
    pieces_in = small_f[...]
    for row, (base, each) in enumerate(SMALL_ROWS):
        piece = each[0] * me + each[1]
        value = jnp.broadcast_to(pieces_in[row : row + 1, :], (16, width))
        value = pltpu.roll(value, (piece % n) * unit, 1)
        placed = placed + jnp.where(row_index == piece // n + base, value, 0.0)
    small_s[0] = placed.astype(LOW)
    grid.greet()

    def small_sum(step, buffer, stage):
        for i, sem in enumerate(stage):
            arrived(buffer.at[i], sem)
        accumulate(
            small_s.at[step + 1], small_s.at[step], *[buffer.at[i] for i in range(len(stage))]
        )

    stage = [
        copies.send(small_s.at[0], small_y.at[k - 1], fsdp=grid.yc(k, 0))
        for k in range(1, grid.y_n)
    ]

    def up_slot(f):
        return wu_s.at[pl.ds(pl.multiple_of(f * up_rows, up_rows), up_rows)]

    up_kept = copies.local(wu_in, up_slot(grid.fsdp))
    up = ShardGather(grid, copies, wu_in, up_slot)
    qkv_sems = []

    def piece_slot(ctx, fsdp, m):
        kind, place = grid.qkv_piece(ctx, fsdp, m)
        return wi_s.at[pl.ds(pl.multiple_of((kind * grid.fsdp_n + place) * unit, unit), unit)]

    for m in range(3):
        user = grid.qkv_user(grid.ctx, grid.fsdp, m)
        qkv_sems.append(
            copies.send_or_keep(
                wq_in.at[pl.ds(m * unit, unit)],
                piece_slot(user, grid.fsdp, m),
                user,
                grid.ctx,
            )
        )
    small_sum(0, small_y, stage)
    stage = [
        copies.send(small_s.at[1], small_x.at[l - 1], ctx=grid.zx(0, l))
        for l in range(1, grid.x_n)
    ]
    tokens_x = TokenGather(grid, copies, x_in, x_s)
    small_sum(1, small_x, stage)
    stage = [
        copies.send(small_s.at[2], small_core.at[c - 1], fsdp=grid.yc(0, c))
        for c in range(1, grid.core_n)
    ]
    small_sum(2, small_core, stage)
    stage = [
        copies.send(small_s.at[3], small_z.at[k - 1], ctx=grid.zx(k, 0))
        for k in range(1, grid.z_n)
    ]

    def column_block(ref, index, block):
        return ref.at[:, pl.ds(pl.multiple_of(index * block, 128), block)]

    mine = wo_s.at[grid.ctx, grid.fsdp]
    own_out = [
        copies.local(column_block(wf_in, grid.ctx, fw), mine.at[:, pl.ds(0, fw)]),
        copies.local(column_block(wd_in, grid.ctx, dw), mine.at[:, pl.ds(fw, dw)]),
    ]
    out_sems = {}

    def send_out(k):
        for l in range(grid.x_n):
            if k or l:
                target = grid.zx(k, l)
                out_sems[k, l] = (
                    copies.send(
                        column_block(wf_in, target, fw), mine.at[:, pl.ds(0, fw)], ctx=target
                    ),
                    copies.send(
                        column_block(wd_in, target, dw), mine.at[:, pl.ds(fw, dw)], ctx=target
                    ),
                )

    shards = []

    def spread_out(k):
        first = ((grid.z - k + grid.z_n) % grid.z_n) * grid.x_n
        for l in range(grid.x_n):
            slot = wo_s.at[grid.zx(-k, -l), grid.fsdp]
            if k or l:
                arrived(slot.at[:, pl.ds(0, fw)], out_sems[k, l][0])
                arrived(slot.at[:, pl.ds(fw, dw)], out_sems[k, l][1])
            else:
                own_out[0].wait()
                own_out[1].wait()

        def out_view(f):
            return wo_s.at[pl.ds(first, grid.x_n), f]

        shards.append(ShardGather(grid, copies, out_view(grid.fsdp), out_view))

    group = grid.x_n * local_len

    def group_rows(first, i, parts):
        place = grid.nearest(first)
        for later in range(first + 1, min(first + 2, grid.z_n)):
            place = jnp.where(i // parts == later - first, grid.nearest(later), place)
        return pl.multiple_of(place * group + (i % parts) * tile_rows, tile_rows)

    def normalize(k):
        first = pl.multiple_of(grid.nearest(k) * group, group)
        gain, shift = small_f[0:1, :], small_f[1:2, :]

        @pl.loop(0, group // 16)
        def _(i):
            rows = pl.ds(pl.multiple_of(first + i * 16, 16), 16)
            wide = x_s[rows, :].astype(F32)
            mean = jnp.mean(wide, axis=-1, keepdims=True)
            centered = wide - mean
            spread = lax.rsqrt(jnp.mean(centered * centered, axis=-1, keepdims=True) + EPSILON)
            normed_s[rows, :] = (centered * spread * gain + shift).astype(LOW)
            lane = lax.broadcasted_iota(jnp.int32, (16, 2 * HEAD_DIM), 1)
            stats_s[rows, :] = jnp.where(lane < HEAD_DIM, mean, spread)

    tile_rows = min(256, group)

    tiles = group // tile_rows

    def project_up(k, groups=1):
        block = min(256, fw)

        @pl.loop(0, groups * tiles * (fw // block))
        def _(i):
            col = (i % (fw // block)) * block
            rows = pl.ds(group_rows(k, i // (fw // block), tiles), tile_rows)
            cols = pl.ds(pl.multiple_of(col, block), block)
            bias = up_bias_s[i % (fw // block), 0:1, :]
            upward = dot_nt(normed_s[rows, :], wu_s[cols, :]) + bias
            square = upward * upward
            bend = jnp.tanh(0.7978845608028654 * (upward + 0.044715 * square * upward))
            half = 0.5 * (1.0 + bend)
            hidden_s[rows, cols] = (upward * half).astype(LOW)
            inner_slope = 0.7978845608028654 * (1.0 + 3.0 * 0.044715 * square)
            slope = half + 0.5 * upward * (1.0 - bend * bend) * inner_slope
            slope_s[rows, cols] = slope.astype(LOW)

    def project_qkv(k, groups=1):
        @pl.loop(0, groups * tiles)
        def _(i):
            start = group_rows(k, i, tiles)
            rows = pl.ds(start, tile_rows)
            for kind in range(3):
                result = dot_nt(normed_s[rows, :], wi_s[kind * dw : (kind + 1) * dw, :])
                result = result + qkv_bias_s[kind, 0:1, :]
                if kind == 2:
                    mixed_s[rows, kind * dw : (kind + 1) * dw] = result.astype(LOW)
                    continue
                for run in range(tile_rows // RUN):
                    tables = run_turn(start_in, step_in, start // RUN + run)
                    run_at = pl.ds(pl.multiple_of(start + run * RUN, RUN), RUN)
                    for p in range(pairs):
                        lanes = slice(p * 2 * HEAD_DIM, (p + 1) * 2 * HEAD_DIM)
                        turned = turn(result[run * RUN : (run + 1) * RUN, lanes], tables)
                        low = turned.astype(LOW)
                        if kind == 0:
                            low = (low * SCORE_SCALE).astype(LOW)
                        at = kind * dw + p * 2 * HEAD_DIM
                        mixed_s[run_at, at : at + 2 * HEAD_DIM] = low

    last = grid.z_n - 1
    tokens_x.step(1)
    send_out(0)
    for k in range(2, last):
        tokens_x.step(k)
        send_out(k - 1)
    tokens_g = TokenGather(grid, copies, g_in, g_s)
    send_out(last - 1)
    tokens_x.step(last)
    send_out(last)
    pieces = []
    for m in range(3):
        arrived(piece_slot(grid.ctx, grid.fsdp, m), qkv_sems[m])
        pieces.append(
            ShardGather(
                grid,
                copies,
                piece_slot(grid.ctx, grid.fsdp, m),
                lambda f, m=m: piece_slot(grid.ctx, f, m),
            )
        )
    up.forward()
    small_sum(3, small_z, stage)
    puts.append(copies.local(small_s.at[4], small_out))
    small_f[...] = small_s[4].astype(F32)
    for kind in range(3):
        at = pl.ds(pl.multiple_of(grid.ctx * dw, 128), dw)
        row = small_f[4 + kind : 5 + kind, at]
        qkv_bias_s[kind] = jnp.broadcast_to(row, qkv_bias_s.shape[1:])
    block = up_bias_s.shape[2]
    for i in range(fw // block):
        offset = grid.ctx * fw
        at = pl.ds(pl.multiple_of(offset % width + i * block, 128), block)
        row = jnp.zeros((1, block), F32)
        for j in range(4):
            row = row + jnp.where(offset // width == j, small_f[7 + j : 8 + j, at], 0.0)
        up_bias_s[i] = jnp.broadcast_to(row, up_bias_s.shape[1:])
    tokens_x.ready(0)
    normalize(0)
    up_kept.wait()
    up.finish()
    puts.append(copies.local(wu_s, wu_out))
    for gather in pieces:
        gather.forward()
    tokens_x.ready(1)
    normalize(1)
    project_up(0, 2)
    for gather in pieces:
        gather.finish()
    puts.append(copies.local(wi_s, wi_out))
    project_qkv(0, 2)
    tokens_g.step(1)
    spread_out(0)
    for k in range(2, grid.z_n):
        tokens_x.ready(k)
        normalize(k)
        project_up(k)
        project_qkv(k)
        spread_out(k - 1)
        shards[k - 2].forward()
        if k == last:
            spread_out(last)
        if k > 2:
            tokens_g.step(k - 1)
    puts.append(copies.local(x_s, x_out))
    puts.append(copies.local(normed_s, normed_out))
    puts.append(copies.local(slope_s, slope_out))
    puts.append(copies.local(stats_s, stats_out))
    length = x_s.shape[0]
    pair = 2 * HEAD_DIM

    tall = min(256, length)

    @pl.loop(0, length // tall)
    def _(i):
        start = pl.multiple_of(i * tall, tall)
        result = dot_nn(to_sorted(row_in, start, tall), mixed_s[...]).astype(LOW)
        for kind in range(3):
            for p in range(pairs):
                at = kind * dw + p * pair
                qkv_s[kind, p, pl.ds(start, tall), :] = result[:, at : at + pair]

    @pl.loop(0, pairs)
    def _(p):
        attend(qkv_s.at[0, p], qkv_s.at[1, p], qkv_s.at[2, p], ctx_s.at[p], lse_s.at[p])

    @pl.loop(0, length // tall)
    def _(i):
        start = pl.multiple_of(i * tall, tall)
        back = to_stored(row_in, start, tall)
        for p in range(pairs):
            at = slice(fw + p * pair, fw + (p + 1) * pair)
            hidden_s[pl.ds(start, tall), at] = dot_tn(back, ctx_s[p]).astype(LOW)

    tokens_g.step(last)
    for gather in shards[last - 1 :]:
        gather.forward()
    puts.append(copies.local(hidden_s, hidden_out))
    puts.append(copies.local(qkv_s, qkv_out))
    puts.append(copies.local(lse_s, lse_out))
    for gather in shards:
        gather.finish()
    puts.append(copies.local(wo_s, wo_out))
    for k in range(grid.z_n):
        tokens_g.ready(k)
    puts.append(copies.local(g_s, g_out))
    for put in puts:
        put.wait()
    copies.drain()


def accumulate(dst, *sources):
    if len(dst.shape) == 3:

        @pl.loop(0, dst.shape[0])
        def _(i):
            accumulate(dst.at[i], *[source.at[i] for source in sources])

        return
    rows, step = dst.shape[0], 16

    @pl.loop(0, rows // step)
    def _(i):
        part = pl.ds(pl.multiple_of(i * step, step), step)
        total = sources[0][part, :].astype(F32)
        for source in sources[1:]:
            total = total + source[part, :].astype(F32)
        dst[part, :] = total.astype(dst.dtype)


class TokenScatter:
    def __init__(self, grid, copies, parts, from_x, from_z, total, half):
        self.grid, self.copies, self.parts = grid, copies, parts
        self.rows = total.shape[0]
        self.cols = pl.ds(half * (total.shape[1] // 2), total.shape[1] // 2)
        self.from_x, self.from_z = from_x.at[:, :, :, self.cols], from_z.at[:, :, self.cols]
        self.total = total.at[:, self.cols]
        self.along_x, self.sems, self.remotes = {}, {}, {}
        self.order = [t for i in range(grid.z_n // 2) for t in (grid.z_n - 1 - i, i)]

    def block(self, t, dx):
        x = (self.grid.x + dx) % self.grid.x_n
        rows = pl.ds(pl.multiple_of(x * self.rows, self.rows), self.rows)
        return self.parts.at[t, rows, self.cols]

    def launch(self, t):
        for l in range(1, self.grid.x_n):
            self.along_x[t, l] = self.copies.send(
                self.block(t, l), self.from_x.at[t, l - 1], ctx=self.grid.zx(0, l)
            )

    def collect(self, t):
        terms = [self.block(t, 0)]
        for l in range(1, self.grid.x_n):
            arrived(self.from_x.at[t, l - 1], self.along_x[t, l])
            terms.append(self.from_x.at[t, l - 1])
        accumulate(terms[0], *terms)

    def hop(self, t, way, first, z):
        grid, own, slot = self.grid, self.block(t, 0), self.from_z.at[t]
        if first:
            after = slot
            if way < 0:
                after = self.from_z.at[jnp.where(grid.z - 1 == t, grid.z_n, t)]
            remote, sem = self.copies.prepare(own, after, ctx=grid.zx(way, 0))
            self.remotes[t, way], self.sems[t, way] = remote, sem
            self.copies.perhaps.append((grid.z < t if way > 0 else grid.z > t, remote))

        @pl.when(grid.z == z)
        def _():
            if not first:
                arrived(slot, self.sems[t, way])
                accumulate(own, own, slot)
            self.remotes[t, way].start()

    def step(self, i):
        last = self.grid.z_n - 1
        if i <= last:
            self.collect(self.order[i])
        for j, t in enumerate(self.order):
            if 0 <= i - j < t:
                self.hop(t, 1, i == j, i - j)
            if 0 <= i - j < last - t:
                self.hop(t, -1, i == j, last - (i - j))

    def finish(self):
        grid = self.grid
        for t in range(grid.z_n):

            @pl.when(grid.z == t)
            def _(t=t):
                terms = [self.block(t, 0)]
                if t > 0:
                    arrived(self.from_z.at[t], self.sems[t, 1])
                    terms.append(self.from_z.at[t])
                if t < grid.z_n - 1:
                    arrived(self.from_z.at[grid.z_n], self.sems[t, -1])
                    terms.append(self.from_z.at[grid.z_n])
                accumulate(self.total, *terms)


class ShardScatter:
    def __init__(self, grid, copies, views, from_core, from_y):
        self.grid, self.copies, self.views = grid, copies, views
        self.from_core, self.from_y = from_core, from_y
        self.rounds = list(range(1, grid.y_n)) + [0]
        self.across = {
            k: [
                copies.send(part, from_core.at[k, i], fsdp=grid.yc(0, 1))
                for i, part in enumerate(views(grid.yc(k, 1)))
            ]
            for k in self.rounds
        }
        self.along_y = {}

    def step(self, k):
        for i, part in enumerate(self.views(self.grid.yc(k, 0))):
            arrived(self.from_core.at[k, i], self.across[k][i])
            accumulate(part, part, self.from_core.at[k, i])
            if k > 0:
                self.along_y[k, i] = self.copies.send(
                    part, self.from_y.at[k - 1, i], fsdp=self.grid.yc(k, 0)
                )

    def finish(self):
        for i, part in enumerate(self.views(self.grid.fsdp)):
            for k in range(1, self.grid.y_n):
                arrived(self.from_y.at[k - 1, i], self.along_y[k, i])
            accumulate(
                part, part, *[self.from_y.at[k - 1, i] for k in range(1, self.grid.y_n)]
            )


def to_sorted(row_ref, start, tile):
    length = row_ref.shape[1]
    place = lax.broadcasted_iota(jnp.int32, (tile, length), 0) + start
    return jnp.where(place == row_ref[0:1, :], 1.0, 0.0).astype(LOW)


def to_stored(row_ref, start, tile):
    length = row_ref.shape[1]
    place = lax.broadcasted_iota(jnp.int32, (length, tile), 0)
    return jnp.where(place == row_ref[0:1, pl.ds(start, tile)], 1.0, 0.0).astype(LOW)


def run_rows(i):
    return pl.ds(pl.multiple_of(i * RUN, RUN), RUN)


def attend_back(q_s, k_s, v_s, lse_s, g_s, dq_s, dk_s, dv_s):
    length = q_s.shape[0]
    dk_s[...] = jnp.zeros_like(dk_s)
    dv_s[...] = jnp.zeros_like(dv_s)
    tile = min(256, length)
    diagonal = lower_triangle(tile)
    for start in range(0, length, tile):
        rows, reach = slice(start, start + tile), start + tile

        @pl.loop(0, 2)
        def _(head, rows=rows, reach=reach, start=start):
            mine = head_lanes(tile, head)
            q_own, g_own = pick(mine, q_s[rows, :]), pick(mine, g_s[rows, :])
            lse = jnp.where(head == 0, lse_s[rows, 0:1], lse_s[rows, HEAD_DIM : HEAD_DIM + 1])
            scores = masked_tile(dot_nt(q_own, k_s[:reach, :]), diagonal, start)
            probs = jnp.exp(scores - lse)
            grad_probs = dot_nt(g_own, v_s[:reach, :])
            inner = jnp.sum(probs * grad_probs, axis=1, keepdims=True)
            grad_scores = (probs * (grad_probs - inner)).astype(LOW)
            grad_q = dot_nn(grad_scores, k_s[:reach, :]) * SCORE_SCALE
            dq_s[rows, :] = jnp.where(mine, grad_q, dq_s[rows, :])
            dk_s[:reach, :] += dot_tn(grad_scores, q_own)
            dv_s[:reach, :] += dot_tn(probs.astype(LOW), g_own)


def scatter_out_kernel(
    shape, hidden_in, wo_in, g_in, slope_in, qkv_in, lse_in,
    row_in, start_in, step_in,
    total_out, go_out, gup_out, gm_out,
    hidden_s, wo_s, g_s, slope_s, qkv_s, lse_s, po_s, po_x, po_z, po_sum,
    go_s, go_core, go_y, gup_s, gctx_s, gm_s, sorted_s, turned_s, dq_s, dk_s, dv_s, sems,
):
    grid = Grid(*shape).locate()
    copies = Copies(sems)
    length, fw = gup_s.shape
    dw = gctx_s.shape[1]
    width, cols = wo_s.shape
    pair = 2 * HEAD_DIM
    loads = [
        copies.local(src, dst)
        for src, dst in (
            (hidden_in, hidden_s), (wo_in, wo_s), (g_in, g_s),
            (slope_in, slope_s), (qkv_in, qkv_s), (lse_in, lse_s),
        )
    ]
    grid.greet()
    loads[0].wait()
    loads[1].wait()
    group = po_s.shape[1]
    tile = min(256, group)
    early, late = (
        TokenScatter(grid, copies, po_s, po_x, po_z, po_sum, half) for half in range(2)
    )
    unit = go_s.shape[2]
    block = grid.fsdp_n * unit
    part_n = grid.ctx_n // 2

    def make_out(first, count=1):
        @pl.loop(0, count * (group // tile) * (width // 256))
        def _(i):
            t, i = first - i // (group // tile * (width // 256)), i % (
                group // tile * (width // 256)
            )
            part = pl.multiple_of((i // (width // 256)) * tile, tile)
            at = pl.ds(pl.multiple_of((i % (width // 256)) * 256, 256), 256)
            rows = pl.ds(pl.multiple_of(t * group + part, tile), tile)
            result = dot_nt(hidden_s[rows, :], wo_s[at, :])
            po_s[t, pl.ds(part, tile), at] = result.astype(LOW)

        for t in range(first, first - count, -1):
            early.launch(t)

    def make_grad_out(part):
        @pl.loop(part * part_n, (part + 1) * part_n)
        def _(c):
            at = pl.ds(pl.multiple_of(c * block, block), block)
            result = dot_tn(g_s[:, at], hidden_s[...]).astype(LOW)
            go_s[c] = result.reshape(grid.fsdp_n, unit, cols)

        span = pl.ds(part * part_n, part_n)
        return ShardScatter(
            grid,
            copies,
            lambda f: [go_s.at[span, f]],
            go_core.at[:, :, span],
            go_y.at[:, :, span],
        )

    make_out(early.order[0])
    make_out(early.order[1])
    loads[2].wait()
    shards = [make_grad_out(0)]
    make_out(grid.z_n - 2, grid.z_n - 2)
    for t in late.order:
        late.launch(t)
    early.step(0)
    shards.append(make_grad_out(1))
    early.step(1)
    for k in shards[0].rounds:
        shards[0].step(k)
    early.step(2)
    for k in shards[1].rounds:
        shards[1].step(k)
    loads[3].wait()
    tall = min(256, length)

    @pl.loop(0, (length // tall) * (fw // 256))
    def _(i):
        rows = pl.ds(pl.multiple_of((i // (fw // 256)) * tall, tall), tall)
        at = pl.ds(pl.multiple_of((i % (fw // 256)) * 256, 256), 256)
        grad = dot_nn(g_s[rows, :], wo_s[:, at])
        gup_s[rows, at] = (grad * slope_s[rows, at].astype(F32)).astype(LOW)

    puts = [copies.local(gup_s, gup_out)]
    early.step(3)

    @pl.loop(0, length // tall)
    def _(i):
        rows = pl.ds(pl.multiple_of(i * tall, tall), tall)
        gctx_s[rows, :] = dot_nn(g_s[rows, :], wo_s[:, pl.ds(fw, dw)]).astype(LOW)

    early.step(grid.z_n)
    late.step(0)
    loads[4].wait()
    loads[5].wait()
    pairs = dw // pair

    @pl.loop(0, length // tall)
    def _(i):
        start = pl.multiple_of(i * tall, tall)
        result = dot_nn(to_sorted(row_in, start, tall), gctx_s[...]).astype(LOW)
        for p in range(pairs):
            sorted_s[p, pl.ds(start, tall), :] = result[:, p * pair : (p + 1) * pair]

    def attend_pairs(first, last):
        @pl.loop(first, last)
        def _(p):
            attend_back(
                qkv_s.at[0, p], qkv_s.at[1, p], qkv_s.at[2, p], lse_s.at[p],
                sorted_s.at[p], dq_s, dk_s, dv_s,
            )

            @pl.loop(0, length // RUN)
            def _(i):
                tables, rows = run_turn(start_in, step_in, i), run_rows(i)
                turned_s[0, p, rows, :] = turn(dq_s[rows, :], tables, -1.0).astype(LOW)
                turned_s[1, p, rows, :] = turn(dk_s[rows, :], tables, -1.0).astype(LOW)
                turned_s[2, p, rows, :] = dv_s[rows, :].astype(LOW)

    late.step(1)
    attend_pairs(0, (pairs + 1) // 2)
    late.step(2)
    late.step(3)
    for shard in shards:
        shard.finish()
    late.step(grid.z_n)
    if pairs > 1:
        attend_pairs((pairs + 1) // 2, pairs)
    puts.append(copies.local(go_s.at[:, grid.fsdp], go_out))

    @pl.loop(0, length // tall)
    def _(i):
        start = pl.multiple_of(i * tall, tall)
        back = to_stored(row_in, start, tall)
        for kind in range(3):
            for p in range(pairs):
                at = kind * dw + p * pair
                result = dot_tn(back, turned_s[kind, p])
                gm_s[pl.ds(start, tall), at : at + pair] = result.astype(LOW)

    puts.append(copies.local(gm_s, gm_out))
    early.finish()
    late.finish()
    puts.append(copies.local(po_sum, total_out))
    for put in puts:
        put.wait()
    copies.drain()


def scatter_in_kernel(
    shape, gm_in, wi_in, gup_in, wu_in, x_in, stats_in, normed_in, g_own_in, go_in,
    total_out, gu_out, gi_out, go_out, small_out,
    gm_s, wi_s, gup_s, wu_s, x_s, stats_s, normed_s, g_own_s, pn_s, pn_x, pn_z, pn_sum,
    gu_s, gu_core, gu_y, gi_s, gi_core, gi_y, gi_got, go_got,
    small_s, small_y, small_x, small_core, small_z, sems,
):
    grid = Grid(*shape).locate()
    copies = Copies(sems)
    length, fw = gup_s.shape
    width = wi_s.shape[1]
    dw = gm_s.shape[1] // 3
    unit = gi_got.shape[1]
    up_rows = fw // grid.fsdp_n
    loads = [
        copies.local(src, dst)
        for src, dst in (
            (gm_in, gm_s), (wi_in, wi_s), (gup_in, gup_s), (wu_in, wu_s),
            (x_in, x_s), (stats_in, stats_s), (normed_in, normed_s), (g_own_in, g_own_s),
        )
    ]
    grid.greet()
    peers = [(k, l) for k in range(grid.z_n) for l in range(grid.x_n) if k or l]
    own_o = copies.local(go_in.at[grid.ctx], go_got.at[grid.ctx])
    out_sems = [
        copies.send(go_in.at[grid.zx(k, l)], go_got.at[grid.ctx], ctx=grid.zx(k, l))
        for k, l in peers
    ]
    small_s[0] = jnp.zeros_like(small_s[0])
    for load in loads[:6]:
        load.wait()
    group = pn_s.shape[1]
    tile = min(256, group)
    early, late = (
        TokenScatter(grid, copies, pn_s, pn_x, pn_z, pn_sum, half) for half in range(2)
    )

    def make_normed(first, count=1):
        @pl.loop(0, count * (group // tile) * (width // 256))
        def _(i):
            t, i = first - i // (group // tile * (width // 256)), i % (
                group // tile * (width // 256)
            )
            part = pl.multiple_of((i // (width // 256)) * tile, tile)
            at = pl.ds(pl.multiple_of((i % (width // 256)) * 256, 256), 256)
            rows = pl.ds(pl.multiple_of(t * group + part, tile), tile)
            grad = dot_nn(gm_s[rows, :], wi_s[:, at]) + dot_nn(gup_s[rows, :], wu_s[:, at])
            pn_s[t, pl.ds(part, tile), at] = grad.astype(LOW)
            mean, spread = stats_s[rows, 0:1], stats_s[rows, HEAD_DIM : HEAD_DIM + 1]
            xhat = (x_s[rows, at].astype(F32) - mean) * spread
            small_s[0, 0:1, at] += jnp.sum(grad * xhat, axis=0, keepdims=True)
            small_s[0, 1:2, at] += jnp.sum(grad, axis=0, keepdims=True)

        for t in range(first, first - count, -1):
            early.launch(t)

    make_normed(early.order[0])
    make_normed(early.order[1])
    for load in loads[6:]:
        load.wait()

    span = width // 2

    @pl.loop(0, 3 * 2)
    def _(i):
        at = pl.ds(pl.multiple_of((i // 2) * dw, dw), dw)
        cols = pl.ds(pl.multiple_of((i % 2) * span, span), span)
        gi_s[at, cols] = dot_tn(gm_s[:, at], normed_s[:, cols]).astype(LOW)

    def piece_slot(f, m):
        kind, place = grid.qkv_piece(grid.ctx, f, m)
        return gi_s.at[pl.ds(pl.multiple_of((kind * grid.fsdp_n + place) * unit, unit), unit)]

    shards_i = ShardScatter(
        grid, copies, lambda f: [piece_slot(f, m) for m in range(3)], gi_core, gi_y
    )
    make_normed(grid.z_n - 2, grid.z_n - 2)
    for t in late.order:
        late.launch(t)

    small_s[0, 2:3, :] = jnp.sum(g_own_s[...].astype(F32), axis=0, keepdims=True)
    for kind in range(3):
        at = pl.ds(pl.multiple_of(grid.ctx * dw, 128), dw)
        terms = gm_s[:, kind * dw : (kind + 1) * dw].astype(F32)
        small_s[0, 4 + kind : 5 + kind, at] = jnp.sum(terms, axis=0, keepdims=True)
    offset = grid.ctx * fw
    at = pl.ds(pl.multiple_of(offset % width, 128), fw)
    terms = jnp.sum(gup_s[...].astype(F32), axis=0, keepdims=True)
    for row in range(4):
        small_s[0, 7 + row : 8 + row, at] = jnp.where(offset // width == row, terms, 0.0)

    def small_sum(step, buffer, stage):
        for i, sem in enumerate(stage):
            arrived(buffer.at[i], sem)
        accumulate(
            small_s.at[step + 1], small_s.at[step], *[buffer.at[i] for i in range(len(stage))]
        )

    stage = [
        copies.send(small_s.at[0], small_y.at[k - 1], fsdp=grid.yc(k, 0))
        for k in range(1, grid.y_n)
    ]

    def up_slot(f):
        return gu_s.at[pl.ds(pl.multiple_of(f * up_rows, up_rows), up_rows)]

    early.step(0)
    for k in shards_i.rounds:
        shards_i.step(k)
    early.step(1)

    @pl.loop(0, fw // 256 * 2)
    def _(i):
        at = pl.ds(pl.multiple_of((i // 2) * 256, 256), 256)
        cols = pl.ds(pl.multiple_of((i % 2) * span, span), span)
        gu_s[at, cols] = dot_tn(gup_s[:, at], normed_s[:, cols]).astype(LOW)

    shards_u = ShardScatter(grid, copies, lambda f: [up_slot(f)], gu_core, gu_y)
    early.step(2)
    small_sum(0, small_y, stage)
    stage = [
        copies.send(small_s.at[1], small_core.at[c - 1], fsdp=grid.yc(0, c))
        for c in range(1, grid.core_n)
    ]
    for k in shards_u.rounds:
        shards_u.step(k)
    early.step(3)
    early.step(grid.z_n)
    late.step(0)
    late.step(1)
    small_sum(1, small_core, stage)
    stage = [
        copies.send(small_s.at[2], small_x.at[l - 1], ctx=grid.zx(0, l))
        for l in range(1, grid.x_n)
    ]
    late.step(2)
    shards_i.finish()
    qkv_sems = []
    for m in range(3):
        owner = grid.qkv_owner(grid.ctx, grid.fsdp, m)
        qkv_sems.append(
            copies.send_or_keep(piece_slot(grid.fsdp, m), gi_got.at[m], owner, grid.ctx)
        )
    late.step(3)
    small_sum(2, small_x, stage)
    stage = [
        copies.send(small_s.at[3], small_z.at[k - 1], ctx=grid.zx(k, 0))
        for k in range(1, grid.z_n)
    ]
    shards_u.finish()
    puts = [copies.local(up_slot(grid.fsdp), gu_out)]
    late.step(grid.z_n)
    early.finish()
    late.finish()
    puts.append(copies.local(pn_sum, total_out))
    own_o.wait()
    for (k, l), sem in zip(peers, out_sems):
        arrived(go_got.at[grid.zx(-k, -l)], sem)
    puts.append(copies.local(go_got, go_out))
    for m in range(3):
        arrived(gi_got.at[m], qkv_sems[m])
    puts.append(copies.local(gi_got, gi_out))
    small_sum(3, small_z, stage)
    puts.append(copies.local(small_s.at[4], small_out))
    for put in puts:
        put.wait()
    copies.drain()


def solution(mesh):
    shape = mesh.shape["ctx"], mesh.shape["fsdp"]
    ctx_n, fsdp_n = shape
    n = ctx_n * fsdp_n
    plan = Grid(*shape)
    x_n, z_n, core_n, y_n = plan.x_n, plan.z_n, plan.core_n, plan.y_n

    def gather(x_own, g_own, w_qkv, w_fc1, w_fc2, w_dense, small, tables):
        local_len, width = x_own.shape
        unit, hidden_units = w_fc2.shape
        length = ctx_n * local_len
        fw, dw = hidden_units // ctx_n, width // ctx_n
        pair = 2 * HEAD_DIM
        small_rows = jax.ShapeDtypeStruct((16, width), LOW)
        kept = [
            jax.ShapeDtypeStruct((length, width), LOW),
            jax.ShapeDtypeStruct((length, width), LOW),
            jax.ShapeDtypeStruct((3 * fsdp_n * unit, width), LOW),
            jax.ShapeDtypeStruct((fw, width), LOW),
            jax.ShapeDtypeStruct((ctx_n, fsdp_n, unit, fw + dw), LOW),
        ]
        made = [
            jax.ShapeDtypeStruct((length, width), LOW),
            jax.ShapeDtypeStruct((length, fw + dw), LOW),
            jax.ShapeDtypeStruct((length, fw), LOW),
            jax.ShapeDtypeStruct((3, dw // pair, length, pair), LOW),
            jax.ShapeDtypeStruct((dw // pair, length, pair), F32),
            jax.ShapeDtypeStruct((length, pair), F32),
        ]
        return pl.pallas_call(
            functools.partial(gather_kernel, shape),
            out_shape=kept + [small_rows] + made,
            in_specs=[anywhere] * 6 + [inside] * 9,
            out_specs=[anywhere] * 12,
            scratch_shapes=[pltpu.VMEM(s.shape, s.dtype) for s in kept + made]
            + [pltpu.VMEM((length, 3 * dw), LOW), pltpu.VMEM((dw // pair, length, pair), LOW)]
            + [pltpu.VMEM((16, width), F32), pltpu.VMEM((3, 8, dw), F32)]
            + [pltpu.VMEM((max(fw // 256, 1), 8, min(fw, 256)), F32)]
            + [pltpu.VMEM((count, 16, width), LOW) for count in (5, x_n, core_n, y_n, z_n)]
            + [pltpu.SemaphoreType.DMA((SEMAPHORES,))],
            compiler_params=pltpu.CompilerParams(
                collective_id=0, has_side_effects=True, vmem_limit_bytes=VMEM_BYTES
            ),
            name="gather",
        )(x_own, g_own, w_qkv, w_fc1, w_fc2, w_dense, *small, *tables)

    def token_scratch(local_len, width):
        return [
            pltpu.VMEM((z_n, x_n * local_len, width), LOW),
            pltpu.VMEM((z_n, max(x_n - 1, 1), local_len, width), LOW),
            pltpu.VMEM((z_n + 1, local_len, width), LOW),
            pltpu.VMEM((local_len, width), F32),
        ]

    def shard_scratch(parts, *block):
        return [
            pltpu.VMEM((y_n, parts) + block, LOW),
            pltpu.VMEM((max(y_n - 1, 1), parts) + block, LOW),
        ]

    def inside_like(*arrays):
        return [pltpu.VMEM(a.shape, a.dtype) for a in arrays]

    anywhere = pl.BlockSpec(memory_space=pl.ANY)
    inside = pl.BlockSpec(memory_space=pltpu.VMEM)

    def scatter_out(hidden, wo, g_all, slope, qkv, lse, tables):
        length, cols = hidden.shape
        local_len, width = length // ctx_n, g_all.shape[1]
        unit = width // n
        fw = slope.shape[1]
        dw, pair = cols - fw, 2 * HEAD_DIM
        return pl.pallas_call(
            functools.partial(scatter_out_kernel, shape),
            out_shape=[
                jax.ShapeDtypeStruct((local_len, width), F32),
                jax.ShapeDtypeStruct((ctx_n, unit, cols), LOW),
                jax.ShapeDtypeStruct((length, fw), LOW),
                jax.ShapeDtypeStruct((length, 3 * dw), LOW),
            ],
            in_specs=[anywhere] * 6 + [inside] * 3,
            out_specs=[anywhere] * 4,
            scratch_shapes=inside_like(hidden, wo, g_all, slope, qkv, lse)
            + token_scratch(local_len, width)
            + [pltpu.VMEM((ctx_n, fsdp_n, unit, cols), LOW)]
            + shard_scratch(1, ctx_n, unit, cols)
            + [pltpu.VMEM((length, c), LOW) for c in (fw, dw, 3 * dw)]
            + [pltpu.VMEM((dw // pair, length, pair), LOW)]
            + inside_like(qkv)
            + [pltpu.VMEM((length, pair), F32)] * 3
            + [pltpu.SemaphoreType.DMA((SEMAPHORES,))],
            compiler_params=pltpu.CompilerParams(
                collective_id=1, has_side_effects=True, vmem_limit_bytes=VMEM_BYTES
            ),
            name="scatter_out",
        )(hidden, wo, g_all, slope, qkv, lse, *tables)

    def scatter_in(gm, wi, gup, wu, x_all, stats, normed, g_own, go):
        length, width = normed.shape
        local_len = length // ctx_n
        unit, up_rows = width // n, wu.shape[0] // fsdp_n
        return pl.pallas_call(
            functools.partial(scatter_in_kernel, shape),
            out_shape=[
                jax.ShapeDtypeStruct((local_len, width), F32),
                jax.ShapeDtypeStruct((up_rows, width), LOW),
                jax.ShapeDtypeStruct((3, unit, width), LOW),
                jax.ShapeDtypeStruct(go.shape, LOW),
                jax.ShapeDtypeStruct((16, width), F32),
            ],
            in_specs=[anywhere] * 9,
            out_specs=[anywhere] * 5,
            scratch_shapes=inside_like(gm, wi, gup, wu, x_all, stats, normed, g_own)
            + token_scratch(local_len, width)
            + inside_like(wu)
            + shard_scratch(1, up_rows, width)
            + inside_like(wi)
            + shard_scratch(3, unit, width)
            + [pltpu.VMEM((3, unit, width), LOW)]
            + inside_like(go)
            + [pltpu.VMEM((count, 16, width), F32) for count in (5, y_n, x_n, core_n, z_n)]
            + [pltpu.SemaphoreType.DMA((SEMAPHORES,))],
            compiler_params=pltpu.CompilerParams(
                collective_id=2, has_side_effects=True, vmem_limit_bytes=VMEM_BYTES
            ),
            name="scatter_in",
        )(gm, wi, gup, wu, x_all, stats, normed, g_own, go)

    def body(
        hidden_in, positions, ln_gain, ln_bias, w_qkv, b_qkv, w_dense, b_dense,
        w_fc1, b_fc1, w_fc2, b_fc2, out_grad,
    ):
        local_len, width = hidden_in.shape[1:]
        hidden_units = w_fc2.shape[1]
        unit = w_dense.shape[0]
        up_rows = w_fc1.shape[0]
        fw, dw = hidden_units // ctx_n, width // ctx_n
        my_ctx = lax.axis_index("ctx")
        me = my_ctx * fsdp_n + lax.axis_index("fsdp")
        length = positions.shape[1]
        x_own, g_own = hidden_in[0], out_grad[0]

        rank = positions[0, ::RUN] // RUN
        starts, steps = turning_tables(length)
        ranks = jnp.arange(length // RUN, dtype=jnp.int32)
        chosen = (rank[:, None] == ranks[None, :])[None, :, :, None]
        stored_starts = jnp.sum(jnp.where(chosen, starts[:, None], 0.0), axis=2)

        own_small = [
            a.reshape(-1, unit) for a in (ln_gain, ln_bias, b_dense, b_fc2, b_qkv, b_fc1)
        ]
        x_all, g_all, wi, wu, wo, small, normed, hidden, slope, qkv, lse, stats = gather(
            x_own, g_own, w_qkv, w_fc1, w_fc2, w_dense, own_small, (positions, stored_starts, steps)
        )
        small = small.astype(F32)
        gain, bias_dense, bias_down = small[0], small[2], small[3]
        total, grad_o, grad_upward, grad_mixed = scatter_out(
            hidden, wo.reshape(width, fw + dw), g_all, slope, qkv, lse, (positions, starts, steps)
        )
        grad_normed, grad_up, grad_qkv, grad_o, sums = scatter_in(
            grad_mixed, wi, grad_upward, wu, x_all, stats, normed, g_own, grad_o
        )

        def standardize(values):
            wide = values.astype(F32)
            centered = wide - jnp.mean(wide, axis=-1, keepdims=True)
            spread = lax.rsqrt(jnp.mean(centered * centered, axis=-1, keepdims=True) + EPSILON)
            return centered * spread, spread

        hidden_out = (total + x_own.astype(F32) + bias_dense + bias_down).astype(LOW)
        xhat, spread = standardize(x_own)
        e = grad_normed * gain
        grad_in = (
            e - jnp.mean(e, axis=-1, keepdims=True)
            - xhat * jnp.mean(e * xhat, axis=-1, keepdims=True)
        ) * spread + g_own.astype(F32)
        grad_o = grad_o.transpose(1, 0, 2).astype(F32)
        sums = sums.reshape(-1)

        def own_slice(row, size):
            return lax.dynamic_slice_in_dim(sums, row * width + me * size, size)

        grad_b_out = own_slice(2, unit)
        return (
            hidden_out[None],
            grad_in[None],
            own_slice(0, unit),
            own_slice(1, unit),
            grad_qkv.reshape(3 * unit, width).astype(F32),
            own_slice(4, 3 * unit),
            grad_o[:, :, fw:].reshape(unit, width),
            grad_b_out,
            grad_up.astype(F32),
            own_slice(7, up_rows),
            grad_o[:, :, :fw].reshape(unit, hidden_units),
            grad_b_out,
        )

    tokens, rows, cells = P("fsdp", "ctx", None), P(BOTH, None), P(BOTH)
    return jax.shard_map(
        body,
        mesh=mesh,
        in_specs=(
            tokens, P("fsdp", None), cells, cells, rows, cells, rows, cells,
            rows, cells, rows, cells, tokens,
        ),
        out_specs=(
            tokens, tokens, cells, cells, rows, cells, rows, cells, rows, cells, rows, cells,
        ),
        check_vma=False,
    )
```

profile of v0, /device:TPU:10, one launch (start us, length us, event | category | flops | bytes accessed | tf_op | source)
XLA Modules:
  0.0 347.0 jit_solution(12682669462603253660)
XLA Ops:
  0.6 0.8 slice.18
  1.4 0.1 iota_compare_fusion
  1.5 1.5 select_reduce_fusion.start_in
  3.0 1.3 reshape.131.bq_in
  4.3 1.3 reshape.132.bu_in
  5.6 130.7 %gather.1 = (bf16[1024,2048]{1,0:T(8,128)(2,1)}, bf16[1024,2048]{1,0:T(8,128)(2,1)}, bf16[768,2048]{1,0:T(8,128)(2,1)}, bf16[1024,2048]{1,0:T(8,128)(2,1)}, bf16...) custom-call(bf16[128,2048]{1,0:T(8,128)(2,1)} %bitcast.41, ...), custom_call_target="tpu_custom_call" | custom-call | tf_op jit(solution)/shard_map/gather/pallas_call | solution.py:1163
  136.3 92.1 %scatter_out.1 = (f32[128,2048]{1,0:T(8,128)}, bf16[8,64,1280]{2,1,0:T(8,128)(2,1)}, bf16[1024,1024]{1,0:T(8,128)(2,1)}, bf16[1024,768]{1,0:T(8,128)(2,1)}) custom-call(bf16[1024,1280]{1,0:T(8,128)(2,1)} %get-tuple-element.33.hidden_in, bf16[2048,1280]{1,0:T(8,128)(2,1)} %bitcast.42, bf16[1024,2048]{1,0:T(8,128)(2,1)} %get-tuple-element.35.g_in, ...), custom_call_target="tpu_custom_call" | custom-call | tf_op jit(solution)/shard_map/scatter_out/pallas_call | solution.py:1206
  228.4 104.9 %scatter_in.1 = (f32[128,2048]{1,0:T(8,128)}, bf16[256,2048]{1,0:T(8,128)(2,1)}, bf16[3,64,2048]{2,1,0:T(8,128)(2,1)}, bf16[8,64,1280]{2,1,0:T(8,128)(2,1)}, f32[16,2048]{1,0:T(8,128)}) custom-call(bf16[1024,768]{1,0:T(8,128)(2,1)} %get-tuple-element.41.gm_in, bf16[768,2048]{1,0:T(8,128)(2,1)} %get-tuple-element.42.wi_in, ...), custom_call_target="tpu_custom_call" | custom-call | tf_op jit(solution)/shard_map/scatter_in/pallas_call | solution.py:1235
  333.3 1.5 convert_bitcast_fusion
  334.8 0.3 slice_bitcast_fusion
  335.1 1.5 copy.33
  336.6 0.0 copy-start.3
  336.6 0.0 copy-start
  336.6 0.8 copy.32
  337.5 0.5 copy-done.3
  338.0 0.0 copy-start.2
  338.0 1.6 convert_element_type.36
  339.5 0.0 copy-start.1
  339.6 0.0 copy-start.4
  339.6 0.9 fusion.15
  340.5 0.0 copy-done
  340.5 0.2 convert_reduce_fusion
  340.7 0.3 fusion.9
  341.0 0.0 copy-done.2
  341.0 0.4 multiply_reduce_fusion
  341.3 0.0 copy-done.1
  341.3 0.0 copy-done.4
  341.3 0.0 copy-start.5
  341.4 1.8 fusion.8
  343.2 0.0 copy-start.6
  343.2 0.0 copy-done.5
  343.2 1.4 bitcast_convert_fusion
  344.6 0.0 copy-done.6
  344.6 0.6 fusion.14
  345.2 0.0 copy-start.7
  345.2 0.6 dynamic_slice.17
  345.9 0.6 dynamic_slice.19
  346.5 0.5 copy.36
  347.0 0.0 copy-done.7
  (6 shorter events, 0.1 us)
Async XLA Ops:
  336.6 1.4 copy-start.3
  336.6 3.9 %copy-start = (bf16[1,128,2048]{2,1,0:T(8,128)(2,1)S(1)}, bf16[1,128,2048]{2,1,0:T(8,128)(2,1)}, u32[]{:S(2)}) copy-start(bf16[1,128,2048]{2,1,0:T(8,128)(2,1)} %param.16) | copy-start | bytes 1572868
  338.0 3.0 copy-start.2
  339.5 1.8 copy-start.1
  339.6 1.8 copy-start.4
  341.3 1.9 copy-start.5
  343.2 1.4 copy-start.6
  345.2 1.8 copy-start.7
where the time goes:
time: 353 us; the launch traced here: 347 us
  Pallas kernels  328 us (93%)
  local copies, waits for them, and re-layouts  9.87 us (3%)
  other arithmetic  8.69 us (2%)
    pallas_call x1, Pallas kernels, gather(): pl.pallas_call(functools.partial(gather_kernel, shape), out_shape=kept +...  131 us
    pallas_call x1, Pallas kernels, scatter_in(): pl.pallas_call(functools.partial(scatter_in_kernel, shape), out_shape=[ja...  105 us
    pallas_call x1, Pallas kernels, scatter_out(): pl.pallas_call(functools.partial(scatter_out_kernel, shape), out_shape=[j...  92.1 us

commit v1 on v0

--- a/solution.py
+++ b/solution.py
@@ -97,8 +97,7 @@
     for start in range(0, length, tile):
         rows, reach = slice(start, start + tile), start + tile
 
-        @pl.loop(0, 2)
-        def _(head, rows=rows, reach=reach, start=start):
+        for head in range(2):
             mine = head_lanes(tile, head)
             scores = dot_nt(pick(mine, q_s[rows, :]), k_s[:reach, :])
             scores = masked_tile(scores, diagonal, start)
@@ -1092,19 +1091,19 @@
     early.step(grid.z_n)
     late.step(0)
     late.step(1)
+    shards_i.finish()
+    qkv_sems = []
+    for m in range(3):
+        owner = grid.qkv_owner(grid.ctx, grid.fsdp, m)
+        qkv_sems.append(
+            copies.send_or_keep(piece_slot(grid.fsdp, m), gi_got.at[m], owner, grid.ctx)
+        )
     small_sum(1, small_core, stage)
     stage = [
         copies.send(small_s.at[2], small_x.at[l - 1], ctx=grid.zx(0, l))
         for l in range(1, grid.x_n)
     ]
     late.step(2)
-    shards_i.finish()
-    qkv_sems = []
-    for m in range(3):
-        owner = grid.qkv_owner(grid.ctx, grid.fsdp, m)
-        qkv_sems.append(
-            copies.send_or_keep(piece_slot(grid.fsdp, m), gi_got.at[m], owner, grid.ctx)
-        )
     late.step(3)
     small_sum(2, small_x, stage)
     stage = [

time: 353 us -> 345 us (0.977); the launches traced: 347 us -> 344 us
  no operation moved by 1% of the time
where the time goes in v1:
time: 345 us; the launch traced here: 344 us
  Pallas kernels  325 us (94%)
  local copies, waits for them, and re-layouts  9.87 us (3%)
  other arithmetic  8.69 us (3%)
    pallas_call x1, Pallas kernels, gather(): pl.pallas_call(functools.partial(gather_kernel, shape), out_shape=kept +...  131 us
    pallas_call x1, Pallas kernels, scatter_in(): pl.pallas_call(functools.partial(scatter_in_kernel, shape), out_shape=[ja...  104 us
    pallas_call x1, Pallas kernels, scatter_out(): pl.pallas_call(functools.partial(scatter_out_kernel, shape), out_shape=[j...  90.5 us

profile of v1, /device:TPU:10, one launch (start us, length us, event | category | flops | bytes accessed | tf_op | source)
XLA Modules:
  0.0 344.4 jit_solution(15206665417206545808)
XLA Ops:
  0.6 0.8 slice.18
  1.4 0.1 iota_compare_fusion
  1.5 1.5 select_reduce_fusion.start_in
  3.0 1.3 reshape.131.bq_in
  4.3 1.3 reshape.132.bu_in
  5.6 130.7 %gather.1 = (bf16[1024,2048]{1,0:T(8,128)(2,1)}, bf16[1024,2048]{1,0:T(8,128)(2,1)}, bf16[768,2048]{1,0:T(8,128)(2,1)}, bf16[1024,2048]{1,0:T(8,128)(2,1)}, bf16...) custom-call(bf16[128,2048]{1,0:T(8,128)(2,1)} %bitcast.41, ...), custom_call_target="tpu_custom_call" | custom-call | tf_op jit(solution)/shard_map/gather/pallas_call | solution.py:1162
  136.3 90.5 %scatter_out.1 = (f32[128,2048]{1,0:T(8,128)}, bf16[8,64,1280]{2,1,0:T(8,128)(2,1)}, bf16[1024,1024]{1,0:T(8,128)(2,1)}, bf16[1024,768]{1,0:T(8,128)(2,1)}) custom-call(bf16[1024,1280]{1,0:T(8,128)(2,1)} %get-tuple-element.33.hidden_in, bf16[2048,1280]{1,0:T(8,128)(2,1)} %bitcast.42, bf16[1024,2048]{1,0:T(8,128)(2,1)} %get-tuple-element.35.g_in, ...), custom_call_target="tpu_custom_call" | custom-call | tf_op jit(solution)/shard_map/scatter_out/pallas_call | solution.py:1205
  226.8 103.8 %scatter_in.1 = (f32[128,2048]{1,0:T(8,128)}, bf16[256,2048]{1,0:T(8,128)(2,1)}, bf16[3,64,2048]{2,1,0:T(8,128)(2,1)}, bf16[8,64,1280]{2,1,0:T(8,128)(2,1)}, f32[16,2048]{1,0:T(8,128)}) custom-call(bf16[1024,768]{1,0:T(8,128)(2,1)} %get-tuple-element.41.gm_in, bf16[768,2048]{1,0:T(8,128)(2,1)} %get-tuple-element.42.wi_in, ...), custom_call_target="tpu_custom_call" | custom-call | tf_op jit(solution)/shard_map/scatter_in/pallas_call | solution.py:1234
  330.6 1.5 convert_bitcast_fusion
  332.2 0.3 slice_bitcast_fusion
  332.4 1.5 copy.33
  333.9 0.0 copy-start.3
  334.0 0.0 copy-start
  334.0 0.8 copy.32
  334.8 0.5 copy-done.3
  335.3 0.0 copy-start.2
  335.3 1.6 convert_element_type.36
  336.9 0.0 copy-start.1
  336.9 0.0 copy-start.4
  336.9 0.9 fusion.15
  337.8 0.0 copy-done
  337.8 0.2 convert_reduce_fusion
  338.0 0.3 fusion.9
  338.3 0.0 copy-done.2
  338.3 0.4 multiply_reduce_fusion
  338.7 0.0 copy-done.1
  338.7 0.0 copy-done.4
  338.7 0.0 copy-start.5
  338.7 1.8 fusion.8
  340.5 0.0 copy-start.6
  340.6 0.0 copy-done.5
  340.6 1.4 bitcast_convert_fusion
  341.9 0.0 copy-done.6
  342.0 0.6 fusion.14
  342.6 0.0 copy-start.7
  342.6 0.6 dynamic_slice.17
  343.2 0.6 dynamic_slice.19
  343.8 0.5 copy.36
  344.3 0.0 copy-done.7
  (6 shorter events, 0.1 us)
Async XLA Ops:
  333.9 1.4 copy-start.3
  334.0 3.9 %copy-start = (bf16[1,128,2048]{2,1,0:T(8,128)(2,1)S(1)}, bf16[1,128,2048]{2,1,0:T(8,128)(2,1)}, u32[]{:S(2)}) copy-start(bf16[1,128,2048]{2,1,0:T(8,128)(2,1)} %param.16) | copy-start | bytes 1572868
  335.3 3.0 copy-start.2
  336.9 1.8 copy-start.1
  336.9 1.8 copy-start.4
  338.7 1.9 copy-start.5
  340.5 1.4 copy-start.6
  342.6 1.8 copy-start.7

commit v2 on v1

--- a/solution.py
+++ b/solution.py
@@ -583,8 +583,8 @@
     for gather in pieces:
         gather.finish()
     puts.append(copies.local(wi_s, wi_out))
+    tokens_g.step(1)
     project_qkv(0, 2)
-    tokens_g.step(1)
     spread_out(0)
     for k in range(2, grid.z_n):
         tokens_x.ready(k)

time: 345 us -> 347 us (level)
  no operation moved by 1% of the time
where the time goes in v2:
time: 347 us
  Pallas kernels  327 us (94%)
  local copies, waits for them, and re-layouts  9.87 us (3%)
  other arithmetic  8.69 us (3%)
    pallas_call x1, Pallas kernels, gather(): pl.pallas_call(functools.partial(gather_kernel, shape), out_shape=kept +...  131 us
    pallas_call x1, Pallas kernels, scatter_in(): pl.pallas_call(functools.partial(scatter_in_kernel, shape), out_shape=[ja...  104 us
    pallas_call x1, Pallas kernels, scatter_out(): pl.pallas_call(functools.partial(scatter_out_kernel, shape), out_shape=[j...  92.8 us

profile of v2, /device:TPU:10, one launch (start us, length us, event | category | flops | bytes accessed | tf_op | source)
XLA Modules:
  0.0 346.7 jit_solution(17534395184288557491)
XLA Ops:
  0.6 0.8 slice.18
  1.4 0.1 iota_compare_fusion
  1.5 1.5 select_reduce_fusion.start_in
  3.0 1.3 reshape.131.bq_in
  4.3 1.3 reshape.132.bu_in
  5.6 130.7 %gather.1 = (bf16[1024,2048]{1,0:T(8,128)(2,1)}, bf16[1024,2048]{1,0:T(8,128)(2,1)}, bf16[768,2048]{1,0:T(8,128)(2,1)}, bf16[1024,2048]{1,0:T(8,128)(2,1)}, bf16...) custom-call(bf16[128,2048]{1,0:T(8,128)(2,1)} %bitcast.41, ...), custom_call_target="tpu_custom_call" | custom-call | tf_op jit(solution)/shard_map/gather/pallas_call | solution.py:1162
  136.3 92.8 %scatter_out.1 = (f32[128,2048]{1,0:T(8,128)}, bf16[8,64,1280]{2,1,0:T(8,128)(2,1)}, bf16[1024,1024]{1,0:T(8,128)(2,1)}, bf16[1024,768]{1,0:T(8,128)(2,1)}) custom-call(bf16[1024,1280]{1,0:T(8,128)(2,1)} %get-tuple-element.33.hidden_in, bf16[2048,1280]{1,0:T(8,128)(2,1)} %bitcast.42, bf16[1024,2048]{1,0:T(8,128)(2,1)} %get-tuple-element.35.g_in, ...), custom_call_target="tpu_custom_call" | custom-call | tf_op jit(solution)/shard_map/scatter_out/pallas_call | solution.py:1205
  229.1 103.8 %scatter_in.1 = (f32[128,2048]{1,0:T(8,128)}, bf16[256,2048]{1,0:T(8,128)(2,1)}, bf16[3,64,2048]{2,1,0:T(8,128)(2,1)}, bf16[8,64,1280]{2,1,0:T(8,128)(2,1)}, f32[16,2048]{1,0:T(8,128)}) custom-call(bf16[1024,768]{1,0:T(8,128)(2,1)} %get-tuple-element.41.gm_in, bf16[768,2048]{1,0:T(8,128)(2,1)} %get-tuple-element.42.wi_in, ...), custom_call_target="tpu_custom_call" | custom-call | tf_op jit(solution)/shard_map/scatter_in/pallas_call | solution.py:1234
  332.9 1.5 convert_bitcast_fusion
  334.5 0.3 slice_bitcast_fusion
  334.8 1.5 copy.33
  336.2 0.0 copy-start.3
  336.3 0.0 copy-start
  336.3 0.8 copy.32
  337.1 0.5 copy-done.3
  337.6 0.0 copy-start.2
  337.6 1.6 convert_element_type.36
  339.2 0.0 copy-start.1
  339.2 0.0 copy-start.4
  339.2 0.9 fusion.15
  340.1 0.0 copy-done
  340.1 0.2 convert_reduce_fusion
  340.3 0.3 fusion.9
  340.6 0.0 copy-done.2
  340.6 0.4 multiply_reduce_fusion
  341.0 0.0 copy-done.1
  341.0 0.0 copy-done.4
  341.0 0.0 copy-start.5
  341.0 1.8 fusion.8
  342.9 0.0 copy-start.6
  342.9 0.0 copy-done.5
  342.9 1.4 bitcast_convert_fusion
  344.2 0.0 copy-done.6
  344.3 0.6 fusion.14
  344.9 0.0 copy-start.7
  344.9 0.6 dynamic_slice.17
  345.5 0.6 dynamic_slice.19
  346.1 0.5 copy.36
  346.7 0.0 copy-done.7
  (6 shorter events, 0.1 us)
Async XLA Ops:
  336.2 1.4 copy-start.3
  336.3 3.9 %copy-start = (bf16[1,128,2048]{2,1,0:T(8,128)(2,1)S(1)}, bf16[1,128,2048]{2,1,0:T(8,128)(2,1)}, u32[]{:S(2)}) copy-start(bf16[1,128,2048]{2,1,0:T(8,128)(2,1)} %param.16) | copy-start | bytes 1572868
  337.6 3.0 copy-start.2
  339.2 1.8 copy-start.1
  339.2 1.8 copy-start.4
  341.0 1.9 copy-start.5
  342.9 1.4 copy-start.6
  344.9 1.8 copy-start.7
